TPU v7x, 32 devices: a whole 2x2x4 slice. The times are simulated.
32 devices in a mesh: section: 8 (over y, x, core), fsdp: 4 (over z).
Axes of the slice: x: 2, y: 2, z: 4, core: 2. Of those that a mesh axis runs over, the one named last changes fastest.
Arguments:
- layer_input: bfloat16 [8, 512, 4096], P('section', 'fsdp'), may hold values from -6 to 6
- next_cot: bfloat16 [8, 512, 512], P('section', 'fsdp'), may hold values from -6 to 6
- w_value: bfloat16 [8, 4096, 512], P('section', 'fsdp'), may hold values from -0.25 to 0.25
- micro_ids: int32 [8, 4], P('section', 'fsdp'), may hold values from 0 to 1
Outputs:
- grad_input: bfloat16 [8, 512, 4096], P('section', 'fsdp')
- grad_sum: float32 [8, 4096, 512], P('section', 'fsdp')
- grad_square: float32 [8, 4096, 512], P('section', 'fsdp')
All inputs are finite; a program needn't handle non-finite values.
Results may differ from a plain program's by a relative error of at most 0.0037.
Values may be sent and summed in bfloat16 or wider, within the bound.
A program may use at most 64 MiB of HBM per device.

v0:
```python
import jax
import jax.numpy as jnp
from jax import lax
from jax.sharding import PartitionSpec as P

MICRO = 2


def from_behind(value, axis, steps):
    count = lax.axis_size(axis)
    pairs = [(source, (source + steps) % count) for source in range(count)]
    return lax.ppermute(value, axis, pairs)


def body(layer_input, next_cot, w_value, micro_ids):
    inputs_local = layer_input[0]
    incoming = from_behind(next_cot, "section", -1)[0]
    weight_local = w_value[0]
    fsdp_count = lax.axis_size("fsdp")
    token_count = inputs_local.shape[0]
    row_share = weight_local.shape[0]
    columns = weight_local.shape[1]
    inverse = 1.0 / token_count
    owned = lax.all_to_all(inputs_local, "fsdp", split_axis=1, concat_axis=0, tiled=True)
    cot_all, micro_all = (
        lax.all_gather(incoming, "fsdp", axis=0, tiled=True),
        lax.all_gather(micro_ids, "fsdp", axis=1, tiled=True),
    )
    owner_cols = lax.dot_general(
        cot_all, weight_local, (((1,), (1,)), ((), ())), preferred_element_type=jnp.float32
    ).astype(jnp.bfloat16)
    grad_input = lax.all_to_all(owner_cols, "fsdp", split_axis=0, concat_axis=1, tiled=True)
    owned = owned.reshape(fsdp_count, token_count, row_share)
    cot_blocks = cot_all.reshape(fsdp_count, token_count, columns)
    partial_value = (
        jnp.einsum("ftd,ftc->fdc", owned, cot_blocks, preferred_element_type=jnp.float32) * inverse
    )
    partial_value = lax.optimization_barrier(partial_value.astype(jnp.bfloat16)).astype(jnp.float32)
    onehot = (micro_all[0][:, None] == jnp.arange(MICRO, dtype=jnp.int32)[None, :]).astype(
        jnp.float32
    )
    stacked = jnp.einsum("fm,fdc->mdc", onehot, partial_value)
    grad_sum = jnp.sum(stacked, axis=0)
    grad_square = jnp.sum(stacked * stacked, axis=0)
    return (grad_input[None], grad_sum[None], grad_square[None])


def solution(mesh):
    return jax.shard_map(
        body,
        mesh=mesh,
        in_specs=(
            P("section", "fsdp", None),
            P("section", "fsdp", None),
            P("section", "fsdp", None),
            P("section", "fsdp"),
        ),
        out_specs=(
            P("section", "fsdp", None),
            P("section", "fsdp", None),
            P("section", "fsdp", None),
        ),
        check_vma=False,
    )
```

profile of v0, /device:TPU:0, one launch (start us, length us, event | category | flops | bytes accessed | tf_op | source)
XLA Modules:
  0.0 94.9 jit_solution(13938566455108437013)
XLA Ops:
  0.6 0.0 copy-start
  0.6 0.0 copy-start.2
  0.7 1.7 %copy.10 = bf16[1,128,4096]{1,2,0:T(8,128)(2,1)S(1)} copy(bf16[1,128,4096]{2,1,0:T(8,128)(2,1)} %param.4) | data formatting | bytes 2097152 | tf_op args[0]
  2.4 1.3 %copy.11 = bf16[128,4,1024]{2,0,1:T(8,128)(2,1)} copy(bf16[128,4,1024]{0,2,1:T(8,128)(2,1)S(1)} %bitcast.25) | data formatting | bytes 2097152 | tf_op jit(solution)/shard_map/all_to_all | solution.py:24
  3.7 0.0 copy-start.3
  3.7 6.5 %all-to-all-start.1 = ((bf16[128,4,1024]{2,0,1:T(8,128)(2,1)}), bf16[128,4,1024]{2,0,1:T(8,128)(2,1)S(1)}, u32[]{:S(2)}, u32[]{:S(2)}) async-start(bf16[128,4,1024]{2,0,1:T(8,128)(2,1)} %copy.11), calls=%async_computation.1 | async-start | bytes 2097152 | tf_op jit(solution)/shard_map/all_to_all | solution.py:24
  10.2 0.0 copy-done.2
  10.2 1.6 %collective-permute-start = (bf16[1,128,512]{2,1,0:T(8,128)(2,1)S(1)}, bf16[1,128,512]{2,1,0:T(8,128)(2,1)S(1)}, u32[]{:S(2)}, u32[]{:S(2)}) collective-permute-start(bf16[1,128,512]{2,1,0:T(8,128)(2,1)S(1)} %copy-done.2), channel_id=1, source_target_pairs={{0,28},{4,0},{8,4},{12,8},{16,12},{20,16},{24,20},{28,24},{1,29},{... | collective-permute-start | bytes 393224 | tf_op jit(solution)/shard_map/ppermute | solution.py:12
  11.8 2.5 %collective-permute-done = bf16[1,128,512]{2,1,0:T(8,128)(2,1)S(1)} collective-permute-done((bf16[1,128,512]{2,1,0:T(8,128)(2,1)S(1)}, bf16[1,128,512]{2,1,0:T(8,128)(2,1)S(1)}, u32[]{:S(2)}, u32[]{:S(2)}) %collective-permute-start) | collective-permute-done | bytes 131104 | tf_op jit(solution)/shard_map/ppermute | solution.py:12
  14.3 32.0 %all-gather = bf16[1,512,512]{2,1,0:T(8,128)(2,1)S(1)} all-gather(bf16[1,128,512]{2,1,0:T(8,128)(2,1)S(1)} %collective-permute-done), channel_id=2, replica_groups=mesh['section'=8,'fsdp'=4] {'fsdp'}, dimensions={1}, use_global_device_ids=true | all-gather | bytes 655360 | tf_op jit(solution)/shard_map/all_gather | solution.py:26
  46.3 0.0 copy-start.1
  46.3 0.8 copy-done.1
  47.1 0.0 copy-done
  47.1 1.7 %convolution_convert_fusion = bf16[512,1024]{1,0:T(8,128)(2,1)} fusion(bf16[1,1024,512]{2,1,0:T(8,128)(2,1)S(1)} %copy-done, bf16[1,512,512]{2,1,0:T(8,128)(2,1)S(1)} %all-gather), kind=kOutput, calls=%fused_computation.4 | convolution fusion | flops 537395200 | bytes 2621440 | tf_op jit(solution)/shard_map/dot_general | solution.py:29
  48.8 0.0 all-to-all-done.1
  48.8 4.6 %all-to-all-start = ((bf16[4,128,1024]{2,1,0:T(8,128)(2,1)}), bf16[4,128,1024]{2,1,0:T(8,128)(2,1)S(1)}, u32[]{:S(2)}, u32[]{:S(2)}) async-start(bf16[4,128,1024]{2,1,0:T(8,128)(2,1)} %bitcast.27), calls=%async_computation | async-start | bytes 2097152 | tf_op jit(solution)/shard_map/all_to_all | solution.py:32
  54.1 0.0 copy-done.3
  54.1 0.6 dynamic-slice
  54.7 0.7 bitcast_dynamic-update-slice_fusion
  55.3 20.2 %all-reduce = s32[4]{0:T(128)S(1)} all-reduce(s32[4]{0:T(128)S(1)} %bitcast_dynamic-update-slice_fusion), channel_id=1, replica_groups=mesh['section'=8,'fsdp'=4] {'fsdp'}, use_global_device_ids=true, to_apply=%add | all-reduce | flops 4 | bytes 32
  75.6 1.3 %copy.12 = bf16[128,4,1024]{0,2,1:T(8,128)(2,1)} copy(bf16[128,4,1024]{2,0,1:T(8,128)(2,1)S(1)} %all-to-all-done.1) | data formatting | bytes 2097152 | tf_op jit(solution)/shard_map/all_to_all | solution.py:24
  76.9 2.6 %multiply_convert_fusion = bf16[4,1024,512]{2,1,0:T(8,128)(2,1)S(1)} fusion(bf16[4,128,512]{2,1,0:T(8,128)(2,1)} %bitcast.26, bf16[128,4,1024]{0,2,1:T(8,128)(2,1)} %copy.12), kind=kOutput, calls=%fused_computation | convolution fusion | flops 541065216 | bytes 5767168 | tf_op jit(solution)/shard_map/ftd,ftc->fdc/dot_general | solution.py:36
  79.4 13.0 %multiply_reduce_fusion = (f32[1024,512]{1,0:T(8,128)}, f32[1024,512]{1,0:T(8,128)}) fusion(bf16[4,1024,512]{2,1,0:T(8,128)(2,1)S(1)} %multiply_convert_fusion, s32[4]{0:T(128)S(1)} %all-reduce), kind=kOutput, calls=%fused_computation.1 | convolution fusion | flops 10485768 | bytes 8388624 | tf_op jit(solution)/shard_map/fm,fdc->mdc/dot_general | solution.py:42
  92.5 0.0 all-to-all-done
  92.5 0.8 copy.9
  93.3 1.6 %broadcast_in_dim.10 = bf16[1,128,4096]{2,1,0:T(8,128)(2,1)} reshape(bf16[128,4,1024]{2,1,0:T(4,128)(2,1)S(1)} %copy.9) | data formatting | bytes 2097152 | tf_op jit(solution)/shard_map/broadcast_in_dim | solution.py:45
  (1 shorter events, 0.0 us)
Async XLA Ops:
  0.6 46.5 %copy-start = (bf16[1,1024,512]{2,1,0:T(8,128)(2,1)S(1)}, bf16[1,1024,512]{2,1,0:T(8,128)(2,1)}, u32[]{:S(2)}) copy-start(bf16[1,1024,512]{2,1,0:T(8,128)(2,1)} %param.6) | copy-start | bytes 3145732
  0.6 9.5 %copy-start.2 = (bf16[1,128,512]{2,1,0:T(8,128)(2,1)S(1)}, bf16[1,128,512]{2,1,0:T(8,128)(2,1)}, u32[]{:S(2)}) copy-start(bf16[1,128,512]{2,1,0:T(8,128)(2,1)} %param.5) | copy-start | bytes 393220
  3.7 50.4 %copy-start.3 = (u32[32]{0:T(128)S(1)}, u32[32]{0:T(128)}, u32[]{:S(2)}) copy-start(u32[32]{0:T(128)} %constant.10) | copy-start | bytes 388
  3.7 45.1 %all-to-all-start.1 = ((bf16[128,4,1024]{2,0,1:T(8,128)(2,1)}), bf16[128,4,1024]{2,0,1:T(8,128)(2,1)S(1)}, u32[]{:S(2)}, u32[]{:S(2)}) async-start(bf16[128,4,1024]{2,0,1:T(8,128)(2,1)} %copy.11), calls=%async_computation.1 | async-start | bytes 2097152 | tf_op jit(solution)/shard_map/all_to_all | solution.py:24
  10.2 4.1 %collective-permute-start = (bf16[1,128,512]{2,1,0:T(8,128)(2,1)S(1)}, bf16[1,128,512]{2,1,0:T(8,128)(2,1)S(1)}, u32[]{:S(2)}, u32[]{:S(2)}) collective-permute-start(bf16[1,128,512]{2,1,0:T(8,128)(2,1)S(1)} %copy-done.2), channel_id=1, source_target_pairs={{0,28},{4,0},{8,4},{12,8},{16,12},{20,16},{24,20},{28,24},{1,29},{... | collective-permute-start | bytes 393224 | tf_op jit(solution)/shard_map/ppermute | solution.py:12
  46.3 0.8 copy-start.1
  48.8 43.7 %all-to-all-start = ((bf16[4,128,1024]{2,1,0:T(8,128)(2,1)}), bf16[4,128,1024]{2,1,0:T(8,128)(2,1)S(1)}, u32[]{:S(2)}, u32[]{:S(2)}) async-start(bf16[4,128,1024]{2,1,0:T(8,128)(2,1)} %bitcast.27), calls=%async_computation | async-start | bytes 2097152 | tf_op jit(solution)/shard_map/all_to_all | solution.py:32
where the time goes:
time: 95.2 us; the launch traced here: 94.9 us
  blocking collectives  52.2 us (55%)
  matrix products  17.4 us (18%)
  starting transfers between devices  12.7 us (13%)
  local copies, waits for them, and re-layouts  8.82 us (9%)
  waiting for transfers between devices  2.53 us (3%)
  between operations  1.34 us (1%)
    all_gather x1, blocking collectives, body(): lax.all_gather(incoming, 'fsdp', axis=0, tiled=True)  32 us
    unnamed x1, blocking collectives  20.2 us
    dot_general x1, matrix products, body(): stacked = jnp.einsum('fm,fdc->mdc', onehot, partial_value)  13 us
    all_to_all x1, starting transfers between devices, body(): lax.all_to_all(inputs_local, 'fsdp', split_axis=1, concat_axis=0, tiled=T...  6.48 us
    all_to_all x1, starting transfers between devices, body(): lax.all_to_all(owner_cols, 'fsdp', split_axis=0, concat_axis=1, tiled=True)  4.58 us
    unnamed x12, local copies, waits for them, and re-layouts  3.8 us
    all_to_all x2, local copies, waits for them, and re-layouts, body(): lax.all_to_all(inputs_local, 'fsdp', split_axis=1, concat_axis=0, tiled=T...  2.61 us
    dot_general x1, matrix products, body(): jnp.einsum('ftd,ftc->fdc', owned, cot_blocks, preferred_element_type=jnp....  2.59 us
  transfers between devices with their start and end apart: 3, of which 1 were waited for; matrix products, arithmetic and copies ran while one was open for 21% of the time, Pallas kernels for 0%

commit v1 on v0

v1 whole, which is shorter than its diff:
```python
import functools

import jax
import jax.numpy as jnp
from jax import lax
from jax.experimental import pallas as pl
from jax.experimental.pallas import tpu as pltpu
from jax.sharding import PartitionSpec as P

MICRO = 2
MESH = pl.DeviceIdType.MESH


def kernel(
    n, ns, li, cot, w, mid, gi, gs, gq,
    inc, lix, gis, ids, wv,
    perm_s, perm_r, right_s, left_s, cot_r, li_s, li_r, gi_s, gi_r, id_s, id_r, own_s,
):
    f = lax.axis_index("fsdp")
    s = lax.axis_index("section")
    behind = lax.rem(s + ns - 1, ns)
    ahead = lax.rem(s + 1, ns)
    tokens, share = lix.shape[1], lix.shape[2]
    columns = inc.shape[2]

    def share_of(ref, part, rows=slice(None)):
        return ref.at[rows, pl.ds(pl.multiple_of(part * share, share), share)]

    def li_copy(target, rows=slice(None)):
        return pltpu.make_async_remote_copy(
            src_ref=share_of(li, target, rows),
            dst_ref=lix.at[f, rows],
            send_sem=li_s.at[target],
            recv_sem=li_r.at[f],
            device_id={"fsdp": target},
            device_id_type=MESH,
        )

    def cot_copy(block, target, sem):
        return pltpu.make_async_remote_copy(
            src_ref=inc.at[block],
            dst_ref=inc.at[block],
            send_sem=sem.at[block],
            recv_sem=cot_r.at[block],
            device_id={"fsdp": target},
            device_id_type=MESH,
        )

    def gi_copy(target):
        return pltpu.make_async_remote_copy(
            src_ref=gis.at[target],
            dst_ref=share_of(gi, f),
            send_sem=gi_s.at[target],
            recv_sem=gi_r.at[f],
            device_id={"fsdp": target},
            device_id_type=MESH,
        )

    def id_copy(target):
        return pltpu.make_async_remote_copy(
            src_ref=ids.at[f],
            dst_ref=ids.at[f],
            send_sem=id_s.at[target],
            recv_sem=id_r.at[f],
            device_id={"fsdp": target},
            device_id_type=MESH,
        )

    weights = pltpu.make_async_copy(w, wv, own_s.at[0])
    weights.start()
    own_li = pltpu.make_async_copy(share_of(li, f), lix.at[f], own_s.at[1])
    own_li.start()
    ids[f] = jnp.full(ids.shape[1:], mid[0, 0], jnp.int32)

    barrier = pltpu.get_barrier_semaphore()
    for peer in (behind, ahead):
        pl.semaphore_signal(barrier, inc=1, device_id={"section": peer}, device_id_type=MESH)
    for step in range(1, n):
        pl.semaphore_signal(
            barrier, inc=1, device_id={"fsdp": lax.rem(f + step, n)}, device_id_type=MESH
        )
    pl.semaphore_wait(barrier, n + 1)

    permute = pltpu.make_async_remote_copy(
        src_ref=cot,
        dst_ref=inc.at[f],
        send_sem=perm_s,
        recv_sem=perm_r,
        device_id={"section": behind},
        device_id_type=MESH,
    )
    permute.start()

    pieces = min(n, 4)
    rows = tokens // pieces

    def li_piece(piece):
        if piece >= pieces:
            return
        window = pl.ds(piece * rows, rows)

        @pl.when(f < n - 1)
        def _():
            li_copy(n - 1, window).start()

        @pl.when(f > 0)
        def _():
            li_copy(0, window).start()

    def forward(step):
        @pl.when((f - step >= 0) & (f < n - 1))
        def _():
            cot_copy(f - step, f + 1, right_s).start()

        @pl.when((f + step < n) & (f > 0))
        def _():
            cot_copy(f + step, f - 1, left_s).start()

    def arrived(step):
        @pl.when(f - step >= 0)
        def _():
            cot_copy(f - step, f, right_s).wait_recv()

        @pl.when(f + step < n)
        def _():
            cot_copy(f + step, f, left_s).wait_recv()

    li_piece(0)
    permute.wait_recv()
    forward(0)
    for step in range(1, n):
        id_copy(lax.rem(f + step, n)).start()
    li_piece(1)
    for step in range(1, n - 1):
        arrived(step)
        forward(step)
        li_piece(step + 1)
    for piece in range(n, pieces):
        li_piece(piece)
    for turn in range(1, n - 1):
        @pl.when(n - 1 - turn > f)
        def _():
            li_copy(n - 1 - turn).start()

        @pl.when(turn < f)
        def _():
            li_copy(turn).start()
    arrived(n - 1)

    weights.wait()

    def input_block(block, carry):
        gis[block] = lax.dot_general(
            inc[block], wv[...], (((1,), (1,)), ((), ())), preferred_element_type=jnp.float32
        ).astype(gis.dtype)
        return carry

    lax.fori_loop(0, n, input_block, 0)
    own_gi = pltpu.make_async_copy(gis.at[f], share_of(gi, f), own_s.at[2])
    own_gi.start()
    for turn in range(n - 1):
        @pl.when(n - 1 - turn > f)
        def _():
            gi_copy(n - 1 - turn).start()

        @pl.when(turn < f)
        def _():
            gi_copy(turn).start()

    own_li.wait()

    def others(action):
        def run(step, carry):
            action(lax.rem(f + step, n))
            return carry

        lax.fori_loop(1, n, run, 0)

    def li_wait(peer):
        pltpu.make_async_remote_copy(
            src_ref=share_of(li, peer),
            dst_ref=lix.at[peer],
            send_sem=li_s.at[peer],
            recv_sem=li_r.at[peer],
            device_id={"fsdp": peer},
            device_id_type=MESH,
        ).wait()
        pltpu.make_async_remote_copy(
            src_ref=ids.at[f],
            dst_ref=ids.at[peer],
            send_sem=id_s.at[peer],
            recv_sem=id_r.at[peer],
            device_id={"fsdp": peer},
            device_id_type=MESH,
        ).wait()

    others(li_wait)

    inverse = 1.0 / tokens
    tile = 128

    def weight_rows(index, carry):
        start = pl.multiple_of(index * tile, tile)
        micro = [jnp.zeros((tile, columns), jnp.float32) for _ in range(MICRO)]
        for block in range(n):
            product = lax.dot_general(
                lix[block, :, pl.ds(start, tile)],
                inc[block],
                (((0,), (0,)), ((), ())),
                preferred_element_type=jnp.float32,
            )
            product = (product * inverse).astype(jnp.bfloat16).astype(jnp.float32)
            owner = jnp.broadcast_to(ids[block][:1, :1], product.shape)
            for m in range(MICRO):
                micro[m] = micro[m] + jnp.where(owner == m, product, 0.0)
        total = micro[0]
        square = micro[0] * micro[0]
        for m in range(1, MICRO):
            total = total + micro[m]
            square = square + micro[m] * micro[m]
        gs[pl.ds(start, tile), :] = total
        gq[pl.ds(start, tile), :] = square
        return carry

    lax.fori_loop(0, share // tile, weight_rows, 0)

    own_gi.wait()
    permute.wait_send()
    for step in range(n - 1):
        @pl.when((f - step >= 0) & (f < n - 1))
        def _():
            cot_copy(f - step, f + 1, right_s).wait_send()

        @pl.when((f + step < n) & (f > 0))
        def _():
            cot_copy(f + step, f - 1, left_s).wait_send()

    def gi_wait(peer):
        pltpu.make_async_remote_copy(
            src_ref=gis.at[peer],
            dst_ref=share_of(gi, peer),
            send_sem=gi_s.at[peer],
            recv_sem=gi_r.at[peer],
            device_id={"fsdp": peer},
            device_id_type=MESH,
        ).wait()

    others(gi_wait)


def body(layer_input, next_cot, w_value, micro_ids):
    n = lax.axis_size("fsdp")
    ns = lax.axis_size("section")
    tokens, width = layer_input.shape[1:]
    share, columns = w_value.shape[1:]
    anywhere = pl.BlockSpec(memory_space=pltpu.HBM)
    dma = pltpu.SemaphoreType.DMA
    grad_input, grad_sum, grad_square = pl.pallas_call(
        functools.partial(kernel, n, ns),
        out_shape=(
            jax.ShapeDtypeStruct((tokens, width), jnp.bfloat16),
            jax.ShapeDtypeStruct((share, columns), jnp.float32),
            jax.ShapeDtypeStruct((share, columns), jnp.float32),
        ),
        in_specs=[anywhere, anywhere, anywhere, pl.BlockSpec(memory_space=pltpu.SMEM)],
        out_specs=OUT_SPECS,
        scratch_shapes=[
            pltpu.VMEM((n, tokens, columns), jnp.bfloat16),
            pltpu.VMEM((n, tokens, share), jnp.bfloat16),
            pltpu.VMEM((n, tokens, share), jnp.bfloat16),
            pltpu.VMEM((n, 8, 128), jnp.int32),
            pltpu.VMEM((share, columns), jnp.bfloat16),
            dma, dma, dma((n,)), dma((n,)), dma((n,)), dma((n,)), dma((n,)),
            dma((n,)), dma((n,)), dma((n,)), dma((n,)), dma((3,)),
        ],
        compiler_params=pltpu.CompilerParams(
            collective_id=0, has_side_effects=True, vmem_limit_bytes=40 * 2**20
        ),
    )(layer_input[0], next_cot[0], w_value[0], micro_ids)
    return (grad_input[None], grad_sum[None], grad_square[None])


OUT_SPECS = (
    pl.BlockSpec(memory_space=pl.ANY),
    pl.BlockSpec(memory_space=pltpu.VMEM),
    pl.BlockSpec(memory_space=pltpu.VMEM),
)


def solution(mesh):
    spec = P("section", "fsdp", None)
    return jax.shard_map(
        body,
        mesh=mesh,
        in_specs=(spec, spec, spec, P("section", "fsdp")),
        out_specs=(spec, spec, spec),
        check_vma=False,
    )
```

time: 95.2 us -> 64.2 us (0.67)
  Pallas kernels: 0 us -> 54.9 us
  blocking collectives: 52.2 us -> 0 us
  matrix products: 17.4 us -> 0 us
  starting transfers between devices: 12.7 us -> 0 us
  waiting for transfers between devices: 2.53 us -> 0 us
  local copies, waits for them, and re-layouts: 8.82 us -> 6.96 us
    pallas_call x0 -> x1, Pallas kernels: none -> 54.9 us  [body(): pl.pallas_call(functools.partial(kernel, n, ns), out_shape=(jax.ShapeDtyp...]
    all_gather x1 -> x0, blocking collectives: 32 us -> none  [body(): lax.all_gather(incoming, 'fsdp', axis=0, tiled=True)]
    unnamed x1 -> x0, blocking collectives: 20.2 us -> none
    dot_general x3 -> x0, matrix products: 17.4 us -> none  [the longest x1 13 us: body(): stacked = jnp.einsum('fm,fdc->mdc', onehot, partial_value)]
    all_to_all x2 -> x0, starting transfers between devices: 11.1 us -> none  [the longest x1 6.48 us: body(): lax.all_to_all(inputs_local, 'fsdp', split_axis=1, concat_axis=0, tiled=T...]
    all_to_all x3 -> x0, local copies, waits for them, and re-layouts: 3.42 us -> none  [the longest x2 2.61 us: body(): lax.all_to_all(inputs_local, 'fsdp', split_axis=1, concat_axis=0, tiled=T...]
    unnamed x12 -> x9, local copies, waits for them, and re-layouts: 3.8 us -> 6.96 us
    ppermute x1 -> x0, waiting for transfers between devices: 2.52 us -> none  [from_behind(): return lax.ppermute(value, axis, pairs)]
  transfers between devices with their start and end apart: 3 -> 0, of which waited for: 1 -> 0; matrix products, arithmetic and copies ran while one was open for 21% -> 0% of each run, Pallas kernels for 0% -> 0%
where the time goes in v1:
time: 64.2 us; the launch traced here: 63.1 us
  Pallas kernels  54.9 us (86%)
  local copies, waits for them, and re-layouts  6.96 us (11%)
  between operations  1.3 us (2%)
    pallas_call x1, Pallas kernels, body(): pl.pallas_call(functools.partial(kernel, n, ns), out_shape=(jax.ShapeDtyp...  54.9 us
    unnamed x9, local copies, waits for them, and re-layouts  6.96 us

profile of v1, /device:TPU:0, one launch (start us, length us, event | category | flops | bytes accessed | tf_op | source)
XLA Modules:
  0.0 63.1 jit_solution(16702294817879992413)
XLA Ops:
  1.3 0.0 copy-start
  1.3 1.2 %copy-done = bf16[1,128,4096]{2,1,0:T(8,128)(2,1)S(1)} copy-done((bf16[1,128,4096]{2,1,0:T(8,128)(2,1)S(1)}, bf16[1,128,4096]{2,1,0:T(8,128)(2,1)}, u32[]{:S(2)}) %copy-start) | copy-done | bytes 1048600
  2.5 0.0 copy-start.1
  2.5 1.2 %copy-done.1 = bf16[1,1024,512]{2,1,0:T(8,128)(2,1)S(1)} copy-done((bf16[1,1024,512]{2,1,0:T(8,128)(2,1)S(1)}, bf16[1,1024,512]{2,1,0:T(8,128)(2,1)}, u32[]{:S(2)}) %copy-start.1) | copy-done | bytes 1048600
  3.7 0.0 copy-start.2
  3.7 0.9 %copy-done.2 = bf16[1,128,512]{2,1,0:T(8,128)(2,1)S(1)} copy-done((bf16[1,128,512]{2,1,0:T(8,128)(2,1)S(1)}, bf16[1,128,512]{2,1,0:T(8,128)(2,1)}, u32[]{:S(2)}) %copy-start.2) | copy-done | bytes 131096
  4.6 54.9 %shard_map.67 = (bf16[128,4096]{1,0:T(8,128)(2,1)S(1)}, f32[1024,512]{1,0:T(8,128)S(1)}, f32[1024,512]{1,0:T(8,128)S(1)}) custom-call(bf16[128,4096]{1,0:T(8,128)(2,1)S(1)} %bitcast.8, bf16[128,512]{1,0:T(8,128)(2,1)S(1)} %bitcast.11, bf16[1024,512]{1,0:T(8,128)(2,1)S(1)} %bitcast.9, s32[1,1]{1,0:T(1,128)S(6)} %copy.10.mid), custom_call_target="tpu_custom_call" | custom-call | tf_op jit(solution)/shard_map/pallas_call | solution.py:258
  59.5 1.0 %copy.11 = bf16[1,128,4096]{2,1,0:T(8,128)(2,1)} copy(bf16[1,128,4096]{2,1,0:T(8,128)(2,1)S(1)} %bitcast.10) | data formatting | bytes 2097152
  60.5 1.3 %copy.12 = f32[1,1024,512]{2,1,0:T(8,128)} copy(f32[1,1024,512]{2,1,0:T(8,128)S(1)} %bitcast.7) | data formatting | bytes 4194304
  61.8 1.3 %copy.13 = f32[1,1024,512]{2,1,0:T(8,128)} copy(f32[1,1024,512]{2,1,0:T(8,128)S(1)} %bitcast.6) | data formatting | bytes 4194304
Async XLA Ops:
  1.3 1.2 %copy-start = (bf16[1,128,4096]{2,1,0:T(8,128)(2,1)S(1)}, bf16[1,128,4096]{2,1,0:T(8,128)(2,1)}, u32[]{:S(2)}) copy-start(bf16[1,128,4096]{2,1,0:T(8,128)(2,1)} %param.4) | copy-start | bytes 3145732
  2.5 1.2 %copy-start.1 = (bf16[1,1024,512]{2,1,0:T(8,128)(2,1)S(1)}, bf16[1,1024,512]{2,1,0:T(8,128)(2,1)}, u32[]{:S(2)}) copy-start(bf16[1,1024,512]{2,1,0:T(8,128)(2,1)} %param.6) | copy-start | bytes 3145732
  3.7 0.9 %copy-start.2 = (bf16[1,128,512]{2,1,0:T(8,128)(2,1)S(1)}, bf16[1,128,512]{2,1,0:T(8,128)(2,1)}, u32[]{:S(2)}) copy-start(bf16[1,128,512]{2,1,0:T(8,128)(2,1)} %param.5) | copy-start | bytes 393220

commit v2 on v1

--- a/solution.py
+++ b/solution.py
@@ -248,6 +248,36 @@
     others(gi_wait)
 
 
+def settle_kernel(cuts, *refs):
+    count = len(refs) // 2
+    sems = refs[-1]
+    copies = []
+    for index in range(count):
+        source, target = refs[index], refs[count + index]
+        rows = source.shape[0] // cuts
+        for cut in range(cuts):
+            window = pl.ds(cut * rows, rows)
+            copies.append(
+                pltpu.make_async_copy(source.at[window], target.at[window], sems.at[index, cut])
+            )
+    for copy in copies:
+        copy.start()
+    for copy in copies:
+        copy.wait()
+
+
+def settle(*arrays):
+    cuts = 1
+    return pl.pallas_call(
+        functools.partial(settle_kernel, cuts),
+        out_shape=tuple(jax.ShapeDtypeStruct(a.shape, a.dtype) for a in arrays),
+        in_specs=[pl.BlockSpec(memory_space=pl.ANY)] * len(arrays),
+        out_specs=tuple(pl.BlockSpec(memory_space=pltpu.HBM) for _ in arrays),
+        scratch_shapes=[pltpu.SemaphoreType.DMA((len(arrays), cuts))],
+        compiler_params=pltpu.CompilerParams(vmem_limit_bytes=4 * 2**20),
+    )(*[pltpu.with_memory_space_constraint(a, pltpu.VMEM) for a in arrays])
+
+
 def body(layer_input, next_cot, w_value, micro_ids):
     n = lax.axis_size("fsdp")
     ns = lax.axis_size("section")
@@ -255,7 +285,8 @@
     share, columns = w_value.shape[1:]
     anywhere = pl.BlockSpec(memory_space=pltpu.HBM)
     dma = pltpu.SemaphoreType.DMA
-    grad_input, grad_sum, grad_square = pl.pallas_call(
+    stay = functools.partial(pltpu.with_memory_space_constraint, memory_space=pltpu.HBM)
+    arrays = pl.pallas_call(
         functools.partial(kernel, n, ns),
         out_shape=(
             jax.ShapeDtypeStruct((tokens, width), jnp.bfloat16),
@@ -276,7 +307,8 @@
         compiler_params=pltpu.CompilerParams(
             collective_id=0, has_side_effects=True, vmem_limit_bytes=40 * 2**20
         ),
-    )(layer_input[0], next_cot[0], w_value[0], micro_ids)
+    )(stay(layer_input[0]), stay(next_cot[0]), stay(w_value[0]), micro_ids)
+    grad_input, grad_sum, grad_square = settle(*arrays)
     return (grad_input[None], grad_sum[None], grad_square[None])
 
 

time: 64.2 us -> 59.7 us (0.930)
  local copies, waits for them, and re-layouts: 6.96 us -> 0 us
  Pallas kernels: 54.9 us -> 57.6 us
    unnamed x9 -> x0, local copies, waits for them, and re-layouts: 6.96 us -> none
    pallas_call x0 -> x1, Pallas kernels: none -> 2.38 us  [settle(): pl.pallas_call(functools.partial(settle_kernel, cuts), out_shape=tuple((j...]
where the time goes in v2:
time: 59.7 us; the launch traced here: 58.9 us
  Pallas kernels  57.6 us (96%)
  between operations  1.29 us (2%)
    pallas_call x1, Pallas kernels, body(): pl.pallas_call(functools.partial(kernel, n, ns), out_shape=(jax.ShapeDtyp...  55.2 us
    pallas_call x1, Pallas kernels, settle(): pl.pallas_call(functools.partial(settle_kernel, cuts), out_shape=tuple((j...  2.38 us

profile of v2, /device:TPU:0, one launch (start us, length us, event | category | flops | bytes accessed | tf_op | source)
XLA Modules:
  0.0 58.9 jit_solution(6708923318009701797)
XLA Ops:
  1.3 55.2 %shard_map.67 = (bf16[128,4096]{1,0:T(8,128)(2,1)S(1)}, f32[1024,512]{1,0:T(8,128)S(1)}, f32[1024,512]{1,0:T(8,128)S(1)}) custom-call(bf16[128,4096]{1,0:T(8,128)(2,1)} %bitcast.6, bf16[128,512]{1,0:T(8,128)(2,1)} %bitcast.8, bf16[1024,512]{1,0:T(8,128)(2,1)} %bitcast.7, s32[1,1]{1,0:T(1,128)S(6)} %copy.7.mid), custom_call_target="tpu_custom_call" | custom-call | tf_op jit(solution)/shard_map/pallas_call | solution.py:289
  56.5 2.4 %shard_map.68 = (bf16[128,4096]{1,0:T(8,128)(2,1)}, f32[1024,512]{1,0:T(8,128)}, f32[1024,512]{1,0:T(8,128)}) custom-call(bf16[128,4096]{1,0:T(8,128)(2,1)S(1)} %get-tuple-element.9.refs_0_, f32[1024,512]{1,0:T(8,128)S(1)} %get-tuple-element.10.refs_1_, f32[1024,512]{1,0:T(8,128)S(1)} %get-tuple-element.11.refs_2_), custom_call_target="tpu_custom_call" | custom-call | tf_op jit(solution)/shard_map/pallas_call | solution.py:271

commit v3 on v2

--- a/solution.py
+++ b/solution.py
@@ -66,20 +66,13 @@
             device_id_type=MESH,
         )
 
-    weights = pltpu.make_async_copy(w, wv, own_s.at[0])
-    weights.start()
-    own_li = pltpu.make_async_copy(share_of(li, f), lix.at[f], own_s.at[1])
-    own_li.start()
-    ids[f] = jnp.full(ids.shape[1:], mid[0, 0], jnp.int32)
-
     barrier = pltpu.get_barrier_semaphore()
-    for peer in (behind, ahead):
-        pl.semaphore_signal(barrier, inc=1, device_id={"section": peer}, device_id_type=MESH)
+    pl.semaphore_signal(barrier, inc=1, device_id={"section": ahead}, device_id_type=MESH)
     for step in range(1, n):
         pl.semaphore_signal(
             barrier, inc=1, device_id={"fsdp": lax.rem(f + step, n)}, device_id_type=MESH
         )
-    pl.semaphore_wait(barrier, n + 1)
+    pl.semaphore_wait(barrier, n)
 
     permute = pltpu.make_async_remote_copy(
         src_ref=cot,
@@ -126,6 +119,11 @@
             cot_copy(f + step, f, left_s).wait_recv()
 
     li_piece(0)
+    weights = pltpu.make_async_copy(w, wv, own_s.at[0])
+    weights.start()
+    own_li = pltpu.make_async_copy(share_of(li, f), lix.at[f], own_s.at[1])
+    own_li.start()
+    ids[f] = jnp.full(ids.shape[1:], mid[0, 0], jnp.int32)
     permute.wait_recv()
     forward(0)
     for step in range(1, n):

time: 59.7 us -> 59.5 us (level); the launches traced: 58.9 us -> 59.3 us
  no operation moved by 1% of the time
where the time goes in v3:
time: 59.5 us; the launch traced here: 59.3 us
  Pallas kernels  58 us (97%)
  between operations  1.29 us (2%)
    pallas_call x1, Pallas kernels, body(): pl.pallas_call(functools.partial(kernel, n, ns), out_shape=(jax.ShapeDtyp...  55.7 us
    pallas_call x1, Pallas kernels, settle(): pl.pallas_call(functools.partial(settle_kernel, cuts), out_shape=tuple((j...  2.38 us

profile of v3, /device:TPU:0, one launch (start us, length us, event | category | flops | bytes accessed | tf_op | source)
XLA Modules:
  0.0 59.3 jit_solution(7142382526622640567)
XLA Ops:
  1.3 55.7 %shard_map.67 = (bf16[128,4096]{1,0:T(8,128)(2,1)S(1)}, f32[1024,512]{1,0:T(8,128)S(1)}, f32[1024,512]{1,0:T(8,128)S(1)}) custom-call(bf16[128,4096]{1,0:T(8,128)(2,1)} %bitcast.6, bf16[128,512]{1,0:T(8,128)(2,1)} %bitcast.8, bf16[1024,512]{1,0:T(8,128)(2,1)} %bitcast.7, s32[1,1]{1,0:T(1,128)S(6)} %copy.7.mid), custom_call_target="tpu_custom_call" | custom-call | tf_op jit(solution)/shard_map/pallas_call | solution.py:287
  56.9 2.4 %shard_map.68 = (bf16[128,4096]{1,0:T(8,128)(2,1)}, f32[1024,512]{1,0:T(8,128)}, f32[1024,512]{1,0:T(8,128)}) custom-call(bf16[128,4096]{1,0:T(8,128)(2,1)S(1)} %get-tuple-element.9.refs_0_, f32[1024,512]{1,0:T(8,128)S(1)} %get-tuple-element.10.refs_1_, f32[1024,512]{1,0:T(8,128)S(1)} %get-tuple-element.11.refs_2_), custom_call_target="tpu_custom_call" | custom-call | tf_op jit(solution)/shard_map/pallas_call | solution.py:269

commit v4 on v3

--- a/solution.py
+++ b/solution.py
@@ -82,7 +82,6 @@
         device_id={"section": behind},
         device_id_type=MESH,
     )
-    permute.start()
 
     pieces = min(n, 4)
     rows = tokens // pieces
@@ -119,6 +118,7 @@
             cot_copy(f + step, f, left_s).wait_recv()
 
     li_piece(0)
+    permute.start()
     weights = pltpu.make_async_copy(w, wv, own_s.at[0])
     weights.start()
     own_li = pltpu.make_async_copy(share_of(li, f), lix.at[f], own_s.at[1])

time: 59.5 us -> 59.5 us (level)
  no operation moved by 1% of the time
where the time goes in v4:
time: 59.5 us; the launch traced here: 59.3 us
  Pallas kernels  58 us (97%)
  between operations  1.29 us (2%)
    pallas_call x1, Pallas kernels, body(): pl.pallas_call(functools.partial(kernel, n, ns), out_shape=(jax.ShapeDtyp...  55.7 us
    pallas_call x1, Pallas kernels, settle(): pl.pallas_call(functools.partial(settle_kernel, cuts), out_shape=tuple((j...  2.38 us

profile of v4, /device:TPU:0, one launch (start us, length us, event | category | flops | bytes accessed | tf_op | source)
XLA Modules:
  0.0 59.3 jit_solution(255376371317480943)
XLA Ops:
  1.3 55.7 %shard_map.67 = (bf16[128,4096]{1,0:T(8,128)(2,1)S(1)}, f32[1024,512]{1,0:T(8,128)S(1)}, f32[1024,512]{1,0:T(8,128)S(1)}) custom-call(bf16[128,4096]{1,0:T(8,128)(2,1)} %bitcast.6, bf16[128,512]{1,0:T(8,128)(2,1)} %bitcast.8, bf16[1024,512]{1,0:T(8,128)(2,1)} %bitcast.7, s32[1,1]{1,0:T(1,128)S(6)} %copy.7.mid), custom_call_target="tpu_custom_call" | custom-call | tf_op jit(solution)/shard_map/pallas_call | solution.py:287
  56.9 2.4 %shard_map.68 = (bf16[128,4096]{1,0:T(8,128)(2,1)}, f32[1024,512]{1,0:T(8,128)}, f32[1024,512]{1,0:T(8,128)}) custom-call(bf16[128,4096]{1,0:T(8,128)(2,1)S(1)} %get-tuple-element.9.refs_0_, f32[1024,512]{1,0:T(8,128)S(1)} %get-tuple-element.10.refs_1_, f32[1024,512]{1,0:T(8,128)S(1)} %get-tuple-element.11.refs_2_), custom_call_target="tpu_custom_call" | custom-call | tf_op jit(solution)/shard_map/pallas_call | solution.py:269
